TPU v7x, 128 devices: a whole 4x4x4 slice. The times are simulated.
128 devices in a mesh: shell: 16 (over z, x), blk: 8 (over y, core).
Axes of the slice: x: 4, y: 4, z: 4, core: 2. Of those that a mesh axis runs over, the one named last changes fastest.
Arguments:
- cycle_fourier: bfloat16 [512, 2, 192, 1024], P('shell', None, None, 'blk'), may hold values from -6 to 6
- legendre: bfloat16 [192, 768, 1024], P('shell', None, 'blk'), may hold values from -0.1875 to 0.1875
- azimuth_orders: int32 [192], replicated, may hold values from 0 to 767, as said below
- multipole: int32 [768], P(('shell', 'blk')), may hold values from 0 to 767, each once
- bessel: bfloat16 [768, 512, 512], P(('shell', 'blk')), may hold values from -0.25 to 0.25
- signal_power: float32 [768, 512], P(('shell', 'blk')), may hold values from 0.1 to 10
- noise_power: float32 [768, 512], P(('shell', 'blk')), may hold values from 0.1 to 10
Outputs:
- filtered: bfloat16 [768, 512, 384], P('shell', 'blk')
Inputs may be any that keep to these rules, and one draw needn't show every extreme that they name: `azimuth_orders`: distinct orders; 0 and 767 always among them. Each multipole 0 to 767 appears once.
All inputs are finite; a program needn't handle non-finite values.
Results may differ from a plain program's by a relative error of at most 0.017.
Values may be sent and summed in bfloat16 or wider, within the bound.
A program may use at most 128 MiB of HBM per device.

v0:
```python
import jax
import jax.numpy as jnp
from jax import lax
from jax.sharding import Mesh, PartitionSpec as P

PLANE = ("z", "x", "y")
ALL = ("z", "x", "y", "core")
SHELL = ("z", "x")
BLK = ("y", "core")


def body(cycle_fourier, legendre, azimuth_orders, multipole, bessel, signal_power, noise_power):
    shells, _, cols, cycles = cycle_fourier.shape
    ny = lax.axis_size("y")
    per = cols // (lax.axis_size("z") * lax.axis_size("x") * ny)
    planes = cols // per
    f = cycle_fourier.transpose(2, 1, 0, 3)
    f = lax.all_to_all(f, PLANE, split_axis=0, concat_axis=0, tiled=True)
    f = f.reshape(planes // ny, ny, per, 2, shells, cycles)
    rows = legendre.shape[1]
    t = lax.all_to_all(legendre, "y", split_axis=0, concat_axis=0, tiled=True)
    t = t.reshape(ny, per, rows, cycles)
    part = jnp.einsum("yjir,ayjcsr->cjias", t, f, preferred_element_type=jnp.float32)
    part = part.astype(jnp.bfloat16).reshape(2, per, rows, planes // ny * shells)
    both = lax.all_to_all(part, "core", split_axis=0, concat_axis=0, tiled=True)
    c = (both[0].astype(jnp.float32) + both[1].astype(jnp.float32)).astype(jnp.bfloat16)
    total = c.shape[-1]
    devices = planes * 2
    local = rows // devices
    c = c.reshape(per, devices, local, total).transpose(1, 2, 0, 3)
    c = lax.all_to_all(c, ALL, split_axis=0, concat_axis=0, tiled=True)
    c = c.reshape(planes, 2, local, per, total).transpose(2, 0, 3, 1, 4)
    coeffs = c.reshape(local, cols, 2, total)
    allowed = multipole[:, None] >= azimuth_orders[None, :]
    coeffs = jnp.where(allowed[:, :, None, None], coeffs, jnp.zeros((), jnp.bfloat16))
    coeffs = coeffs.reshape(local, cols * 2, total)
    forward = jnp.einsum("iks,ijs->ikj", bessel, coeffs, preferred_element_type=jnp.float32)
    wiener = signal_power / (signal_power + noise_power)
    scaled = (forward * wiener[:, :, None]).astype(jnp.bfloat16)
    out = jnp.einsum("iks,ikj->isj", bessel, scaled, preferred_element_type=jnp.float32)
    return lax.all_to_all(out.astype(jnp.bfloat16), BLK, split_axis=1, concat_axis=0, tiled=True)


def solution(mesh):
    fine = Mesh(mesh.devices.reshape(4, 4, 4, 2), ALL)
    return jax.shard_map(
        body,
        mesh=fine,
        in_specs=(
            P(SHELL, None, None, BLK),
            P(SHELL, None, BLK),
            P(),
            P(ALL),
            P(ALL, None, None),
            P(ALL, None),
            P(ALL, None),
        ),
        out_specs=P(SHELL, BLK, None),
        check_vma=False,
    )
```

profile of v0, /device:TPU:1, one launch (start us, length us, event | category | flops | bytes accessed | tf_op | source)
XLA Modules:
  0.0 224.5 jit_solution(8660560980968956102)
XLA Ops:
  0.0 5.3 %all-to-all-start.1 = ((bf16[12,768,128]{2,1,0:T(8,128)(2,1)}), bf16[12,768,128]{2,1,0:T(8,128)(2,1)}, u32[]{:S(2)}, u32[]{:S(2)}) async-start(bf16[12,768,128]{2,1,0:T(8,128)(2,1)} %param.8), calls=%async_computation.1 | async-start | bytes 4718592 | tf_op jit(solution)/shard_map/all_to_all | solution.py:21
  5.3 5.6 %copy.49 = bf16[32,2,192,128]{3,0,1,2:T(8,128)(2,1)} copy(bf16[32,2,192,128]{3,2,1,0:T(8,128)(2,1)} %param.7) | data formatting | bytes 6291456 | tf_op args[0]
  10.8 23.3 %all-to-all-done.1 = bf16[12,768,128]{2,1,0:T(8,128)(2,1)} async-done(((bf16[12,768,128]{2,1,0:T(8,128)(2,1)}), bf16[12,768,128]{2,1,0:T(8,128)(2,1)}, u32[]{:S(2)}, u32[]{:S(2)}) %all-to-all-start.1) | async-done | bytes 2359328 | tf_op jit(solution)/shard_map/all_to_all | solution.py:21
  34.1 48.1 %all_to_all.38 = bf16[192,2,32,128]{3,2,1,0:T(8,128)(2,1)S(1)} all-to-all(bf16[192,2,32,128]{3,2,1,0:T(8,128)(2,1)} %bitcast.32), channel_id=1, replica_groups=mesh['z'=4,'x'=4,'y'=4,'core'=2] {'z','x','y'}, dimensions={0} | all-to-all | bytes 6291456 | tf_op jit(solution)/shard_map/all_to_all | solution.py:18
  82.2 4.6 %fusion = bf16[2,3,768,16,32]{2,4,0,3,1:T(8,128)(2,1)S(1)} fusion(bf16[16,4,3,2,32,128]{5,4,3,2,1,0:T(8,128)(2,1)S(1)} %bitcast.36, bf16[4,3,768,128,1,1]{3,2,1,0,5,4:T(8,128)(2,1)} %bitcast.3), kind=kOutput, calls=%fused_computation.1 | convolution fusion | flops 2418278400 | bytes 10223616 | tf_op jit(solution)/shard_map/yjir,ayjcsr->cjias/dot_general | solution.py:23
  86.8 0.5 copy.28
  87.3 10.5 %all_to_all.39 = bf16[2,3,768,512]{2,3,1,0:T(8,128)(2,1)S(1)} all-to-all(bf16[2,3,768,512]{2,3,1,0:T(8,128)(2,1)S(1)} %bitcast.31), channel_id=1, replica_groups=mesh['z'=4,'x'=4,'y'=4,'core'=2] {'core'}, dimensions={0} | all-to-all | bytes 9437184 | tf_op jit(solution)/shard_map/all_to_all | solution.py:25
  97.7 1.9 add_convert_fusion
  99.7 4.3 %copy.29 = bf16[1,3,768,512]{3,2,1,0:T(8,128)(2,1)} copy(bf16[1,3,768,512]{2,3,1,0:T(8,128)(2,1)} %add_convert_fusion) | data formatting | bytes 4718592 | tf_op jit(solution)/shard_map/convert_element_type | solution.py:26
  104.0 5.0 %convert_element_type.38 = bf16[3,128,6,512]{3,2,1,0:T(8,128)(2,1)} reshape(bf16[1,3,768,512]{3,2,1,0:T(8,128)(2,1)} %copy.29) | data formatting | bytes 4718592 | tf_op jit(solution)/shard_map/convert_element_type | solution.py:26
  109.0 3.8 %copy.30 = bf16[128,6,3,512]{3,1,2,0:T(8,128)(2,1)} copy(bf16[128,6,3,512]{3,1,0,2:T(8,128)(2,1)} %bitcast.33) | data formatting | bytes 4718592 | tf_op jit(solution)/shard_map/transpose | solution.py:30
  112.8 5.0 %all-to-all-start.3 = ((bf16[128,6,3,512]{3,1,2,0:T(8,128)(2,1)}), bf16[128,6,3,512]{3,1,2,0:T(8,128)(2,1)}, u32[]{:S(2)}, u32[]{:S(2)}) async-start(bf16[128,6,3,512]{3,1,2,0:T(8,128)(2,1)} %copy.30), calls=%async_computation.3 | async-start | bytes 6291456 | tf_op jit(solution)/shard_map/all_to_all | solution.py:31
  117.9 0.0 copy-done.3
  117.9 0.0 copy-done.4
  117.9 0.1 broadcast_compare_fusion
  118.0 0.2 broadcast_in_dim.20
  118.2 0.4 broadcast_in_dim.21
  118.6 40.7 %all-to-all-done.3 = bf16[128,6,3,512]{3,1,2,0:T(8,128)(2,1)} async-done(((bf16[128,6,3,512]{3,1,2,0:T(8,128)(2,1)}), bf16[128,6,3,512]{3,1,2,0:T(8,128)(2,1)}, u32[]{:S(2)}, u32[]{:S(2)}) %all-to-all-start.3) | async-done | bytes 2359328 | tf_op jit(solution)/shard_map/all_to_all | solution.py:31
  159.3 5.1 %copy.50 = bf16[64,2,6,3,512]{4,1,3,0,2:T(2,128)(2,1)} copy(bf16[64,2,6,3,512]{4,2,3,1,0:T(8,128)(2,1)} %bitcast.9) | data formatting | bytes 4718592 | tf_op jit(solution)/shard_map/transpose | solution.py:32
  164.5 6.1 %reshape.57 = bf16[6,384,512]{2,1,0:T(8,128)(2,1)} reshape(bf16[6,64,3,2,512]{4,3,2,1,0:T(2,128)(2,1)} %bitcast.35) | data formatting | bytes 4718592 | tf_op jit(solution)/shard_map/reshape | solution.py:33
  170.6 5.2 %convert_bitcast_fusion = bf16[6,512,384]{1,2,0:T(8,128)(2,1)} fusion(bf16[6,512,512]{2,1,0:T(8,128)(2,1)S(1)} %copy-done, f32[6,512]{1,0:T(8,128)S(1)} %add_divide_fusion, bf16[6,384,512]{2,1,0:T(8,128)(2,1)} %reshape.57, pred[6,384]{1,0:T(8,128)(4,1)S(1)} %broadcast_in_dim.21), kind=kOutput, calls=%fused_computation.9 | convolution fusion | flops 2420637696 | bytes 7878912 | tf_op jit(solution)/shard_map/iks,ikj->isj/dot_general | solution.py:40
  175.8 4.8 %copy.33 = bf16[6,512,384]{2,0,1:T(8,128)(2,1)} copy(bf16[6,512,384]{1,2,0:T(8,128)(2,1)} %convert_bitcast_fusion) | data formatting | bytes 4718592 | tf_op jit(solution)/shard_map/convert_element_type | solution.py:41
  180.6 42.0 %all_to_all.40 = bf16[6,512,384]{2,0,1:T(8,128)(2,1)S(1)} all-to-all(bf16[6,512,384]{2,0,1:T(8,128)(2,1)} %copy.33), channel_id=1, replica_groups=mesh['z'=4,'x'=4,'y'=4,'core'=2] {'y','core'}, dimensions={1} | all-to-all | bytes 4718592 | tf_op jit(solution)/shard_map/all_to_all | solution.py:41
  222.6 1.9 copy.35
  (9 shorter events, 0.0 us)
Async XLA Ops:
  0.0 170.6 %copy-start = (bf16[6,512,512]{2,1,0:T(8,128)(2,1)S(1)}, bf16[6,512,512]{2,1,0:T(8,128)(2,1)}, u32[]{:S(2)}) copy-start(bf16[6,512,512]{2,1,0:T(8,128)(2,1)} %param.11) | copy-start | bytes 9437188
  0.0 34.1 %all-to-all-start.1 = ((bf16[12,768,128]{2,1,0:T(8,128)(2,1)}), bf16[12,768,128]{2,1,0:T(8,128)(2,1)}, u32[]{:S(2)}, u32[]{:S(2)}) async-start(bf16[12,768,128]{2,1,0:T(8,128)(2,1)} %param.8), calls=%async_computation.1 | async-start | bytes 4718592 | tf_op jit(solution)/shard_map/all_to_all | solution.py:21
  112.8 5.0 %copy-start.3 = (s32[192]{0:T(256)S(1)}, s32[192]{0:T(256)}, u32[]{:S(2)}) copy-start(s32[192]{0:T(256)} %param.9) | copy-start | bytes 2308
  112.8 5.0 %copy-start.4 = (s32[6]{0:T(128)S(1)}, s32[6]{0:T(128)}, u32[]{:S(2)}) copy-start(s32[6]{0:T(128)} %param.10) | copy-start | bytes 76
  112.8 5.8 %copy-start.1 = (f32[6,512]{1,0:T(8,128)S(1)}, f32[6,512]{1,0:T(8,128)}, u32[]{:S(2)}) copy-start(f32[6,512]{1,0:T(8,128)} %param.12) | copy-start | bytes 36868
  112.8 5.8 %copy-start.2 = (f32[6,512]{1,0:T(8,128)S(1)}, f32[6,512]{1,0:T(8,128)}, u32[]{:S(2)}) copy-start(f32[6,512]{1,0:T(8,128)} %param.13) | copy-start | bytes 36868
  112.8 46.5 %all-to-all-start.3 = ((bf16[128,6,3,512]{3,1,2,0:T(8,128)(2,1)}), bf16[128,6,3,512]{3,1,2,0:T(8,128)(2,1)}, u32[]{:S(2)}, u32[]{:S(2)}) async-start(bf16[128,6,3,512]{3,1,2,0:T(8,128)(2,1)} %copy.30), calls=%async_computation.3 | async-start | bytes 6291456 | tf_op jit(solution)/shard_map/all_to_all | solution.py:31
where the time goes:
time: 226 us; the launch traced here: 224 us
  blocking collectives  101 us (45%)
  waiting for transfers between devices  64 us (28%)
  local copies, waits for them, and re-layouts  37.8 us (17%)
  starting transfers between devices  10.3 us (5%)
  matrix products  9.76 us (4%)
    all_to_all x1, blocking collectives, body(): f = lax.all_to_all(f, PLANE, split_axis=0, concat_axis=0, tiled=True)  48.1 us
    all_to_all x1, blocking collectives, body(): lax.all_to_all(out.astype(jnp.bfloat16), BLK, split_axis=1, concat_axis=0...  42 us
    all_to_all x1, waiting for transfers between devices, body(): c = lax.all_to_all(c, ALL, split_axis=0, concat_axis=0, tiled=True)  40.7 us
    all_to_all x1, waiting for transfers between devices, body(): t = lax.all_to_all(legendre, 'y', split_axis=0, concat_axis=0, tiled=True)  23.3 us
    all_to_all x1, blocking collectives, body(): both = lax.all_to_all(part, 'core', split_axis=0, concat_axis=0, tiled=True)  10.5 us
    convert_element_type x2, local copies, waits for them, and re-layouts, body(): (both[0].astype(jnp.float32) + both[1].astype(jnp.float32)).astype(jnp.bf...  9.36 us
    reshape x1, local copies, waits for them, and re-layouts, body(): coeffs = c.reshape(local, cols, 2, total)  6.12 us
    unnamed x11, local copies, waits for them, and re-layouts  5.57 us
  transfers between devices with their start and end apart: 2, of which 2 were waited for; matrix products, arithmetic and copies ran while one was open for 3% of the time, Pallas kernels for 0%

commit v1 on v0

--- a/solution.py
+++ b/solution.py
@@ -7,6 +7,12 @@
 ALL = ("z", "x", "y", "core")
 SHELL = ("z", "x")
 BLK = ("y", "core")
+
+
+def exchange_blocks(x, axis, split, join):
+    parts = jnp.split(x, lax.axis_size(axis), axis=split)
+    arrived = lax.all_to_all(jnp.stack(parts), axis, 0, 0)
+    return jnp.concatenate(arrived, axis=join)
 
 
 def body(cycle_fourier, legendre, azimuth_orders, multipole, bessel, signal_power, noise_power):
@@ -38,7 +44,7 @@
     wiener = signal_power / (signal_power + noise_power)
     scaled = (forward * wiener[:, :, None]).astype(jnp.bfloat16)
     out = jnp.einsum("iks,ikj->isj", bessel, scaled, preferred_element_type=jnp.float32)
-    return lax.all_to_all(out.astype(jnp.bfloat16), BLK, split_axis=1, concat_axis=0, tiled=True)
+    return exchange_blocks(out.astype(jnp.bfloat16), BLK, 1, 0)
 
 
 def solution(mesh):

time: 226 us -> 229 us (1.013)
  local copies, waits for them, and re-layouts: 37.8 us -> 49.6 us
  blocking collectives: 101 us -> 92.1 us
    unnamed x11 -> x21, local copies, waits for them, and re-layouts: 5.57 us -> 17 us
    all_to_all x1, blocking collectives: 42 us -> 33.5 us  [exchange_blocks(): arrived = lax.all_to_all(jnp.stack(parts), axis, 0, 0)]
    another operation x0 -> x2, local copies, waits for them, and re-layouts: none -> 7.07 us  [exchange_blocks(): arrived = lax.all_to_all(jnp.stack(parts), axis, 0, 0)]
    convert_element_type x1 -> x0, local copies, waits for them, and re-layouts: 4.8 us -> none  [body(): out.astype(jnp.bfloat16)]
where the time goes in v1:
time: 229 us; the launch traced here: 228 us
  blocking collectives  92.1 us (40%)
  waiting for transfers between devices  64 us (28%)
  local copies, waits for them, and re-layouts  49.6 us (22%)
  starting transfers between devices  10.3 us (4%)
  matrix products  9.76 us (4%)
    all_to_all x1, blocking collectives, body(): f = lax.all_to_all(f, PLANE, split_axis=0, concat_axis=0, tiled=True)  48.1 us
    all_to_all x1, waiting for transfers between devices, body(): c = lax.all_to_all(c, ALL, split_axis=0, concat_axis=0, tiled=True)  40.7 us
    all_to_all x1, blocking collectives, exchange_blocks(): arrived = lax.all_to_all(jnp.stack(parts), axis, 0, 0)  33.5 us
    all_to_all x1, waiting for transfers between devices, body(): t = lax.all_to_all(legendre, 'y', split_axis=0, concat_axis=0, tiled=True)  23.3 us
    unnamed x21, local copies, waits for them, and re-layouts  17 us
    all_to_all x1, blocking collectives, body(): both = lax.all_to_all(part, 'core', split_axis=0, concat_axis=0, tiled=True)  10.5 us
    convert_element_type x2, local copies, waits for them, and re-layouts, body(): (both[0].astype(jnp.float32) + both[1].astype(jnp.float32)).astype(jnp.bf...  9.35 us
    another operation x2, local copies, waits for them, and re-layouts, exchange_blocks(): arrived = lax.all_to_all(jnp.stack(parts), axis, 0, 0)  7.07 us
  transfers between devices with their start and end apart: 2, of which 2 were waited for; matrix products, arithmetic and copies ran while one was open for 3% of the time, Pallas kernels for 0%

profile of v1, /device:TPU:1, one launch (start us, length us, event | category | flops | bytes accessed | tf_op | source)
XLA Modules:
  0.0 227.8 jit_solution(16882216143470103210)
XLA Ops:
  0.0 5.3 %all-to-all-start.1 = ((bf16[12,768,128]{2,1,0:T(8,128)(2,1)}), bf16[12,768,128]{2,1,0:T(8,128)(2,1)}, u32[]{:S(2)}, u32[]{:S(2)}) async-start(bf16[12,768,128]{2,1,0:T(8,128)(2,1)} %param.8), calls=%async_computation.1 | async-start | bytes 4718592 | tf_op jit(solution)/shard_map/all_to_all | solution.py:27
  5.3 5.5 %copy.45 = bf16[32,2,192,128]{3,0,1,2:T(8,128)(2,1)} copy(bf16[32,2,192,128]{3,2,1,0:T(8,128)(2,1)} %param.7) | data formatting | bytes 6291456 | tf_op args[0]
  10.8 23.3 %all-to-all-done.1 = bf16[12,768,128]{2,1,0:T(8,128)(2,1)} async-done(((bf16[12,768,128]{2,1,0:T(8,128)(2,1)}), bf16[12,768,128]{2,1,0:T(8,128)(2,1)}, u32[]{:S(2)}, u32[]{:S(2)}) %all-to-all-start.1) | async-done | bytes 2359328 | tf_op jit(solution)/shard_map/all_to_all | solution.py:27
  34.1 48.1 %all_to_all.25 = bf16[192,2,32,128]{3,2,1,0:T(8,128)(2,1)S(1)} all-to-all(bf16[192,2,32,128]{3,2,1,0:T(8,128)(2,1)} %bitcast.61), channel_id=1, replica_groups=mesh['z'=4,'x'=4,'y'=4,'core'=2] {'z','x','y'}, dimensions={0} | all-to-all | bytes 6291456 | tf_op jit(solution)/shard_map/all_to_all | solution.py:24
  82.2 4.6 %fusion = bf16[2,3,768,16,32]{2,4,0,3,1:T(8,128)(2,1)S(1)} fusion(bf16[16,4,3,2,32,128]{5,4,3,2,1,0:T(8,128)(2,1)S(1)} %bitcast.65, bf16[4,3,768,128,1,1]{3,2,1,0,5,4:T(8,128)(2,1)} %bitcast.3), kind=kOutput, calls=%fused_computation.1 | convolution fusion | flops 2418278400 | bytes 10223616 | tf_op jit(solution)/shard_map/yjir,ayjcsr->cjias/dot_general | solution.py:29
  87.3 10.5 %all_to_all.26 = bf16[2,3,768,512]{2,3,1,0:T(8,128)(2,1)S(1)} all-to-all(bf16[2,3,768,512]{2,3,1,0:T(8,128)(2,1)S(1)} %bitcast.60), channel_id=1, replica_groups=mesh['z'=4,'x'=4,'y'=4,'core'=2] {'core'}, dimensions={0} | all-to-all | bytes 9437184 | tf_op jit(solution)/shard_map/all_to_all | solution.py:31
  97.7 1.9 add_convert_fusion
  99.7 4.3 %copy.28 = bf16[1,3,768,512]{3,2,1,0:T(8,128)(2,1)} copy(bf16[1,3,768,512]{2,3,1,0:T(8,128)(2,1)} %add_convert_fusion) | data formatting | bytes 4718592 | tf_op jit(solution)/shard_map/convert_element_type | solution.py:32
  104.0 5.0 %convert_element_type.38 = bf16[3,128,6,512]{3,2,1,0:T(8,128)(2,1)} reshape(bf16[1,3,768,512]{3,2,1,0:T(8,128)(2,1)} %copy.28) | data formatting | bytes 4718592 | tf_op jit(solution)/shard_map/convert_element_type | solution.py:32
  109.0 3.8 %copy.29 = bf16[128,6,3,512]{3,1,2,0:T(8,128)(2,1)} copy(bf16[128,6,3,512]{3,1,0,2:T(8,128)(2,1)} %bitcast.62) | data formatting | bytes 4718592 | tf_op jit(solution)/shard_map/transpose | solution.py:36
  112.8 5.0 %all-to-all-start.3 = ((bf16[128,6,3,512]{3,1,2,0:T(8,128)(2,1)}), bf16[128,6,3,512]{3,1,2,0:T(8,128)(2,1)}, u32[]{:S(2)}, u32[]{:S(2)}) async-start(bf16[128,6,3,512]{3,1,2,0:T(8,128)(2,1)} %copy.29), calls=%async_computation.3 | async-start | bytes 6291456 | tf_op jit(solution)/shard_map/all_to_all | solution.py:37
  118.6 40.7 %all-to-all-done.3 = bf16[128,6,3,512]{3,1,2,0:T(8,128)(2,1)} async-done(((bf16[128,6,3,512]{3,1,2,0:T(8,128)(2,1)}), bf16[128,6,3,512]{3,1,2,0:T(8,128)(2,1)}, u32[]{:S(2)}, u32[]{:S(2)}) %all-to-all-start.3) | async-done | bytes 2359328 | tf_op jit(solution)/shard_map/all_to_all | solution.py:37
  159.3 5.1 %copy.46 = bf16[64,2,6,3,512]{4,1,3,0,2:T(2,128)(2,1)} copy(bf16[64,2,6,3,512]{4,2,3,1,0:T(8,128)(2,1)} %bitcast.9) | data formatting | bytes 4718592 | tf_op jit(solution)/shard_map/transpose | solution.py:38
  164.4 6.1 %reshape.60 = bf16[6,384,512]{2,1,0:T(8,128)(2,1)} reshape(bf16[6,64,3,2,512]{4,3,2,1,0:T(2,128)(2,1)} %bitcast.64) | data formatting | bytes 4718592 | tf_op jit(solution)/shard_map/reshape | solution.py:39
  170.6 5.2 %convert_bitcast_fusion = bf16[6,512,384]{1,2,0:T(8,128)(2,1)} fusion(bf16[6,512,512]{2,1,0:T(8,128)(2,1)S(1)} %copy-done, f32[6,512]{1,0:T(8,128)S(1)} %add_divide_fusion, bf16[6,384,512]{2,1,0:T(8,128)(2,1)} %reshape.60, pred[6,384]{1,0:T(8,128)(4,1)S(1)} %broadcast_in_dim.21), kind=kOutput, calls=%fused_computation.9 | convolution fusion | flops 2420637696 | bytes 7878912 | tf_op jit(solution)/shard_map/iks,ikj->isj/dot_general | solution.py:46
  175.7 2.1 fusion.21
  177.8 2.1 fusion.20
  179.9 1.9 fusion.19
  181.9 1.0 fusion.18
  183.8 1.0 fusion.16
  185.8 1.1 fusion.14
  186.8 6.0 %copy.32 = bf16[8,6,64,384]{3,2,1,0:T(8,128)(2,1)} copy(bf16[8,6,64,384]{2,3,1,0:T(8,128)(2,1)} %fusion.14) | data formatting | bytes 4718592 | tf_op jit(solution)/shard_map/stack | solution.py:14
  192.9 33.5 %all_to_all.27 = bf16[8,6,64,384]{3,2,1,0:T(8,128)(2,1)S(1)} all-to-all(bf16[8,6,64,384]{3,2,1,0:T(8,128)(2,1)} %copy.32), channel_id=1, replica_groups=mesh['z'=4,'x'=4,'y'=4,'core'=2] {'y','core'}, dimensions={0} | all-to-all | bytes 4718592 | tf_op jit(solution)/shard_map/all_to_all | solution.py:14
  226.4 1.4 copy.55
  (19 shorter events, 3.1 us)
Async XLA Ops:
  0.0 170.6 %copy-start = (bf16[6,512,512]{2,1,0:T(8,128)(2,1)S(1)}, bf16[6,512,512]{2,1,0:T(8,128)(2,1)}, u32[]{:S(2)}) copy-start(bf16[6,512,512]{2,1,0:T(8,128)(2,1)} %param.11) | copy-start | bytes 9437188
  0.0 34.1 %all-to-all-start.1 = ((bf16[12,768,128]{2,1,0:T(8,128)(2,1)}), bf16[12,768,128]{2,1,0:T(8,128)(2,1)}, u32[]{:S(2)}, u32[]{:S(2)}) async-start(bf16[12,768,128]{2,1,0:T(8,128)(2,1)} %param.8), calls=%async_computation.1 | async-start | bytes 4718592 | tf_op jit(solution)/shard_map/all_to_all | solution.py:27
  112.8 5.0 %copy-start.4 = (s32[192]{0:T(256)S(1)}, s32[192]{0:T(256)}, u32[]{:S(2)}) copy-start(s32[192]{0:T(256)} %param.9) | copy-start | bytes 2308
  112.8 5.0 %copy-start.5 = (s32[6]{0:T(128)S(1)}, s32[6]{0:T(128)}, u32[]{:S(2)}) copy-start(s32[6]{0:T(128)} %param.10) | copy-start | bytes 76
  112.8 5.8 %copy-start.2 = (f32[6,512]{1,0:T(8,128)S(1)}, f32[6,512]{1,0:T(8,128)}, u32[]{:S(2)}) copy-start(f32[6,512]{1,0:T(8,128)} %param.12) | copy-start | bytes 36868
  112.8 5.8 %copy-start.3 = (f32[6,512]{1,0:T(8,128)S(1)}, f32[6,512]{1,0:T(8,128)}, u32[]{:S(2)}) copy-start(f32[6,512]{1,0:T(8,128)} %param.13) | copy-start | bytes 36868
  112.8 46.5 %all-to-all-start.3 = ((bf16[128,6,3,512]{3,1,2,0:T(8,128)(2,1)}), bf16[128,6,3,512]{3,1,2,0:T(8,128)(2,1)}, u32[]{:S(2)}, u32[]{:S(2)}) async-start(bf16[128,6,3,512]{3,1,2,0:T(8,128)(2,1)} %copy.29), calls=%async_computation.3 | async-start | bytes 6291456 | tf_op jit(solution)/shard_map/all_to_all | solution.py:37
  175.7 6.1 %copy-start.1 = (bf16[6,512,384]{1,2,0:T(8,128)(2,1)S(1)}, bf16[6,512,384]{1,2,0:T(8,128)(2,1)}, u32[]{:S(2)}) copy-start(bf16[6,512,384]{1,2,0:T(8,128)(2,1)} %convert_bitcast_fusion) | copy-start | bytes 7077892
